TPU v7x, 32 devices: a whole 2x2x4 slice. The times are simulated.
32 devices in a mesh: grp: 4 (over x, core), mem: 8 (over z, y).
Axes of the slice: x: 2, y: 2, z: 4, core: 2. Of those that a mesh axis runs over, the one named last changes fastest.
Arguments:
- history: bfloat16 [16384, 256], P(('grp', 'mem')), may hold values from -6 to 6
- tiles: bfloat16 [20480, 128, 128], P(('grp', 'mem')), may hold values from -0.0390625 to 0.0390625
- tile_row: int32 [20480], P(('grp', 'mem')), may hold values from 0 to 31
- tile_col: int32 [20480], P(('grp', 'mem')), may hold values from 0 to 31
- weight: bfloat16 [256, 256], replicated, may hold values from -0.375 to 0.375
- bias: float32 [256], replicated, may hold values from -3 to 3
- cotangent: bfloat16 [16384, 256], P(('grp', 'mem')), may hold values from -0.046875 to 0.046875
Outputs:
- activation: bfloat16 [16384, 256], P(('grp', 'mem'))
- weight_grad: float32 [256, 256], replicated
- bias_grad: float32 [256], replicated
All inputs are finite; a program needn't handle non-finite values.
Results may differ from a plain program's by a relative error of at most 0.012.
Values may be sent and summed in bfloat16 or wider, within the bound.
No kernel may reach another device: no remote copies, remote signals or barrier semaphores. Data moves between devices by JAX's collectives and lax.ppermute only.
A program may use at most 128 MiB of HBM per device.

v0:
```python
import math
import jax
import jax.numpy as jnp
from jax import lax
from jax.sharding import PartitionSpec as P


def per_device(history, tiles, tile_row, tile_col, weight, bias, cotangent):
    own_rows = history.shape[0]
    block = tiles.shape[1]
    width = history.shape[1]
    group = lax.all_gather(history, "mem", axis=0, tiled=True)
    nblk = group.shape[0] // block
    flat_blocks = group.reshape(nblk, block * width)
    step = math.gcd(tiles.shape[0], 64)
    count = tiles.shape[0] // step
    block_ids = lax.broadcasted_iota(jnp.int32, (step, nblk), 1)

    def accumulate(index, dense):
        start = index * step
        piece = lax.dynamic_slice_in_dim(tiles, start, step, 0)
        rows = lax.dynamic_slice_in_dim(tile_row, start, step, 0)
        cols = lax.dynamic_slice_in_dim(tile_col, start, step, 0)
        col_table = (cols[:, None] == block_ids).astype(jnp.bfloat16)
        row_table = (rows[:, None] == block_ids).astype(jnp.bfloat16)
        picked = jnp.dot(col_table, flat_blocks, preferred_element_type=jnp.float32).astype(
            jnp.bfloat16
        )
        picked = picked.reshape(step, block, width)
        part = jnp.einsum("tij,tjh->tih", piece, picked, preferred_element_type=jnp.float32)
        part = part.reshape(step, block * width)
        upper = part.astype(jnp.bfloat16)
        lower = (part - upper.astype(jnp.float32)).astype(jnp.bfloat16)
        contract = (((0,), (0,)), ((), ()))
        added = lax.dot_general(row_table, upper, contract, preferred_element_type=jnp.float32)
        added = added + lax.dot_general(
            row_table, lower, contract, preferred_element_type=jnp.float32
        )
        return dense + added

    dense = lax.fori_loop(0, count, accumulate, jnp.zeros((nblk, block * width), jnp.float32))
    flat = dense.reshape(nblk * block, width)
    total = lax.psum(flat, "mem")
    summed = lax.dynamic_slice_in_dim(total, lax.axis_index("mem") * own_rows, own_rows, 0)
    merged = summed.astype(jnp.bfloat16)
    pre = jnp.dot(merged, weight, preferred_element_type=jnp.float32) + bias
    sig = jax.nn.sigmoid(pre)
    activation = (pre * sig).astype(jnp.bfloat16)
    slope = sig * (1.0 + pre * (1.0 - sig))
    masked = (cotangent.astype(jnp.float32) * slope).astype(jnp.bfloat16)
    local_grad = lax.dot_general(
        merged, masked, (((0,), (0,)), ((), ())), preferred_element_type=jnp.float32
    )
    local_bias = jnp.sum(masked.astype(jnp.float32), axis=0)
    weight_grad, bias_grad = lax.psum((local_grad, local_bias), ("grp", "mem"))
    return (activation, weight_grad, bias_grad)


def solution(mesh):
    placed = (
        P(("grp", "mem"), None),
        P(("grp", "mem"), None, None),
        P(("grp", "mem")),
        P(("grp", "mem")),
        P(),
        P(),
        P(("grp", "mem"), None),
    )
    return jax.shard_map(
        per_device,
        mesh=mesh,
        in_specs=placed,
        out_specs=(P(("grp", "mem"), None), P(), P()),
        check_vma=False,
    )
```

profile of v0, /device:TPU:0, one launch (start us, length us, event | category | flops | bytes accessed | tf_op | source)
XLA Modules:
  0.0 637.3 jit_solution(10937932440289297246)
XLA Ops:
  8.0 54.0 %all-gather.2.cloned.1.call-done = bf16[4096,256]{1,0:T(8,128)(2,1)} async-done(((bf16[512,256]{1,0:T(8,128)(2,1)}), bf16[4096,256]{1,0:T(8,128)(2,1)}) %all-gather.2.cloned.1.call-update) | async-done | bytes 2097168 | tf_op jit(solution)/shard_map/all_gather | solution.py:12
  62.0 2.9 reshape.29
  64.8 266.7 %while.15 = (s32[]{:T(128)}, f32[32,32768]{1,0:T(8,128)}, s32[640]{0:T(1024)}, bf16[640,128,128]{2,1,0:T(8,128)(2,1)}, s32[640]{0:T(1024)}, /*index=5*/bf16[32,3...) while((s32[]{:T(128)}, f32[32,32768]{1,0:T(8,128)}, ...), condition=%wide.region_1.0_spmd.clone.clone, body=%wide.region_0.0_spmd.clone.clone.sunk | while | flops 955258880 | bytes 113248200 | solution.py:41
  65.6 1.3 convolution_convert_fusion.2
  66.9 1.1 copy.14
  68.0 2.9 fusion.30
  70.9 4.7 copy.15
  76.4 3.5 fusion.31
  80.2 10.3 %fusion.32 = f32[32,32768]{1,0:T(8,128)} fusion(f32[32,32768]{1,0:T(8,128)} %fusion.31, f32[64,32768]{1,0:T(8,128)} %bitcast.21, f32[32,32768]{1,0:T(8,128)} %get-tuple-element.235, pred[]{:T(512)S(6)} %compare.3, s32[64]{0:T(128)S(1)} %dynamic_slice.43), kind=kOutput, calls=%fused_computation.3.clone.1 | convolution fusion | flops 145754112 | bytes 20971776 | tf_op jit(solution)/shard_map/while/body/eval_jaxpr/dot_general | solution.py:36
  91.2 1.3 convolution_convert_fusion.2
  92.5 1.1 copy.14
  93.6 2.9 fusion.30
  96.5 4.7 copy.15
  102.0 3.5 fusion.31
  105.8 11.5 %fusion.32 = f32[32,32768]{1,0:T(8,128)} fusion(f32[32,32768]{1,0:T(8,128)} %fusion.31, f32[64,32768]{1,0:T(8,128)} %bitcast.21, f32[32,32768]{1,0:T(8,128)} %get-tuple-element.235, pred[]{:T(512)S(6)} %compare.3, s32[64]{0:T(128)S(1)} %dynamic_slice.43), kind=kOutput, calls=%fused_computation.3.clone.1 | convolution fusion | flops 145754112 | bytes 20971776 | tf_op jit(solution)/shard_map/while/body/eval_jaxpr/dot_general | solution.py:36
  118.0 1.3 convolution_convert_fusion.2
  120.4 2.9 fusion.30
  123.3 4.7 copy.15
  128.8 3.5 fusion.31
  132.6 11.5 %fusion.32 = f32[32,32768]{1,0:T(8,128)} fusion(f32[32,32768]{1,0:T(8,128)} %fusion.31, f32[64,32768]{1,0:T(8,128)} %bitcast.21, f32[32,32768]{1,0:T(8,128)} %get-tuple-element.235, pred[]{:T(512)S(6)} %compare.3, s32[64]{0:T(128)S(1)} %dynamic_slice.43), kind=kOutput, calls=%fused_computation.3.clone.1 | convolution fusion | flops 145754112 | bytes 20971776 | tf_op jit(solution)/shard_map/while/body/eval_jaxpr/dot_general | solution.py:36
  144.8 1.3 convolution_convert_fusion.2
  146.1 1.1 copy.14
  147.2 2.9 fusion.30
  150.1 4.7 copy.15
  155.6 3.5 fusion.31
  159.4 11.5 %fusion.32 = f32[32,32768]{1,0:T(8,128)} fusion(f32[32,32768]{1,0:T(8,128)} %fusion.31, f32[64,32768]{1,0:T(8,128)} %bitcast.21, f32[32,32768]{1,0:T(8,128)} %get-tuple-element.235, pred[]{:T(512)S(6)} %compare.3, s32[64]{0:T(128)S(1)} %dynamic_slice.43), kind=kOutput, calls=%fused_computation.3.clone.1 | convolution fusion | flops 145754112 | bytes 20971776 | tf_op jit(solution)/shard_map/while/body/eval_jaxpr/dot_general | solution.py:36
  171.6 1.3 convolution_convert_fusion.2
  172.9 1.1 copy.14
  174.0 2.9 fusion.30
  176.8 4.7 copy.15
  182.4 3.5 fusion.31
  186.1 11.5 %fusion.32 = f32[32,32768]{1,0:T(8,128)} fusion(f32[32,32768]{1,0:T(8,128)} %fusion.31, f32[64,32768]{1,0:T(8,128)} %bitcast.21, f32[32,32768]{1,0:T(8,128)} %get-tuple-element.235, pred[]{:T(512)S(6)} %compare.3, s32[64]{0:T(128)S(1)} %dynamic_slice.43), kind=kOutput, calls=%fused_computation.3.clone.1 | convolution fusion | flops 145754112 | bytes 20971776 | tf_op jit(solution)/shard_map/while/body/eval_jaxpr/dot_general | solution.py:36
  198.4 1.3 convolution_convert_fusion.2
  200.8 2.9 fusion.30
  203.6 4.7 copy.15
  209.2 3.5 fusion.31
  212.9 11.5 %fusion.32 = f32[32,32768]{1,0:T(8,128)} fusion(f32[32,32768]{1,0:T(8,128)} %fusion.31, f32[64,32768]{1,0:T(8,128)} %bitcast.21, f32[32,32768]{1,0:T(8,128)} %get-tuple-element.235, pred[]{:T(512)S(6)} %compare.3, s32[64]{0:T(128)S(1)} %dynamic_slice.43), kind=kOutput, calls=%fused_computation.3.clone.1 | convolution fusion | flops 145754112 | bytes 20971776 | tf_op jit(solution)/shard_map/while/body/eval_jaxpr/dot_general | solution.py:36
  225.2 1.3 convolution_convert_fusion.2
  226.5 1.1 copy.14
  227.6 2.9 fusion.30
  230.4 4.7 copy.15
  236.0 3.5 fusion.31
  239.7 11.5 %fusion.32 = f32[32,32768]{1,0:T(8,128)} fusion(f32[32,32768]{1,0:T(8,128)} %fusion.31, f32[64,32768]{1,0:T(8,128)} %bitcast.21, f32[32,32768]{1,0:T(8,128)} %get-tuple-element.235, pred[]{:T(512)S(6)} %compare.3, s32[64]{0:T(128)S(1)} %dynamic_slice.43), kind=kOutput, calls=%fused_computation.3.clone.1 | convolution fusion | flops 145754112 | bytes 20971776 | tf_op jit(solution)/shard_map/while/body/eval_jaxpr/dot_general | solution.py:36
  251.9 1.3 convolution_convert_fusion.2
  254.3 2.9 fusion.30
  257.2 4.7 copy.15
  262.8 3.5 fusion.31
  266.5 11.5 %fusion.32 = f32[32,32768]{1,0:T(8,128)} fusion(f32[32,32768]{1,0:T(8,128)} %fusion.31, f32[64,32768]{1,0:T(8,128)} %bitcast.21, f32[32,32768]{1,0:T(8,128)} %get-tuple-element.235, pred[]{:T(512)S(6)} %compare.3, s32[64]{0:T(128)S(1)} %dynamic_slice.43), kind=kOutput, calls=%fused_computation.3.clone.1 | convolution fusion | flops 145754112 | bytes 20971776 | tf_op jit(solution)/shard_map/while/body/eval_jaxpr/dot_general | solution.py:36
  278.7 1.3 convolution_convert_fusion.2
  281.1 2.9 fusion.30
  284.0 4.7 copy.15
  289.6 3.5 fusion.31
  293.3 11.5 %fusion.32 = f32[32,32768]{1,0:T(8,128)} fusion(f32[32,32768]{1,0:T(8,128)} %fusion.31, f32[64,32768]{1,0:T(8,128)} %bitcast.21, f32[32,32768]{1,0:T(8,128)} %get-tuple-element.235, pred[]{:T(512)S(6)} %compare.3, s32[64]{0:T(128)S(1)} %dynamic_slice.43), kind=kOutput, calls=%fused_computation.3.clone.1 | convolution fusion | flops 145754112 | bytes 20971776 | tf_op jit(solution)/shard_map/while/body/eval_jaxpr/dot_general | solution.py:36
  305.5 1.3 convolution_convert_fusion.2
  307.9 2.9 fusion.30
  310.8 4.7 copy.15
  316.3 3.5 fusion.31
  320.1 11.5 %fusion.32 = f32[32,32768]{1,0:T(8,128)} fusion(f32[32,32768]{1,0:T(8,128)} %fusion.31, f32[64,32768]{1,0:T(8,128)} %bitcast.21, f32[32,32768]{1,0:T(8,128)} %get-tuple-element.235, pred[]{:T(512)S(6)} %compare.3, s32[64]{0:T(128)S(1)} %dynamic_slice.43), kind=kOutput, calls=%fused_computation.3.clone.1 | convolution fusion | flops 145754112 | bytes 20971776 | tf_op jit(solution)/shard_map/while/body/eval_jaxpr/dot_general | solution.py:36
  331.6 4.9 reshape.30
  336.4 165.1 %all-reduce.4 = bf16[4096,256]{1,0:T(8,128)(2,1)S(1)} all-reduce(f32[4096,256]{1,0:T(8,128)} %reshape.30), channel_id=1, replica_groups=mesh['grp'=4,'mem'=8] {'mem'}, use_global_device_ids=true, to_apply=%region_2.0 | all-reduce | flops 1048576 | bytes 6291456 | tf_op jit(solution)/shard_map/psum | solution.py:43
  501.6 1.1 convert_reduce_fusion
  503.7 39.3 %psum.23 = f32[256]{0:T(256)} all-reduce(f32[256]{0:T(256)S(1)} %get-tuple-element.184), channel_id=1, replica_groups=mesh['grp'=4,'mem'=8] {'grp','mem'}, use_global_device_ids=true, to_apply=%region_5.0 | all-reduce | flops 256 | bytes 2048 | tf_op jit(solution)/shard_map/psum | solution.py:55
  543.1 85.7 %all-reduce.3.cloned.1.call-done = f32[256,256]{1,0:T(8,128)} async-done(((f32[256,256]{1,0:T(8,128)}), f32[256,256]{1,0:T(8,128)}) %all-reduce.3.cloned.1.call-update) | async-done | bytes 262160 | tf_op jit(solution)/shard_map/psum | solution.py:55
  628.7 1.7 copy.25
  (57 shorter events, 25.9 us)
Async XLA Ops:
  7.2 494.4 %copy-start = (bf16[256,256]{1,0:T(8,128)(2,1)S(1)}, bf16[256,256]{1,0:T(8,128)(2,1)}, u32[]{:S(2)}) copy-start(bf16[256,256]{1,0:T(8,128)(2,1)} %param.13) | copy-start | bytes 393220
  7.2 54.8 %all-gather.2.cloned.1.call-start = ((), (), s32[]{:S(2)}) async-start(), calls=%async_computation | async-start | bytes 2359296 | tf_op jit(solution)/shard_map/all_gather | solution.py:12
  7.9 620.8 %all-reduce.3.cloned.1.call-start = ((), (), s32[]{:S(2)}) async-start(), calls=%async_computation.1 | async-start | bytes 524288 | tf_op jit(solution)/shard_map/psum | solution.py:55
  75.6 4.6 copy-start.1
  101.2 4.6 copy-start.1
  128.0 4.6 copy-start.1
  154.8 4.6 copy-start.1
  181.6 4.6 copy-start.1
  208.4 4.6 copy-start.1
  235.2 4.6 copy-start.1
  261.9 4.6 copy-start.1
  288.7 4.6 copy-start.1
  315.5 4.6 copy-start.1
  336.4 165.2 %copy-start.2 = (bf16[512,256]{1,0:T(8,128)(2,1)S(1)}, bf16[512,256]{1,0:T(8,128)(2,1)}, u32[]{:S(2)}) copy-start(bf16[512,256]{1,0:T(8,128)(2,1)} %param.15) | copy-start | bytes 786436
  336.4 165.2 %copy-start.3 = (f32[256]{0:T(256)S(1)}, f32[256]{0:T(256)}, u32[]{:S(2)}) copy-start(f32[256]{0:T(256)} %param.14) | copy-start | bytes 3076
Sparse Core Ops, SparseCore 0:
  10.1 51.7 all-gather.1
  503.9 124.8 all-reduce.2
where the time goes:
time: 639 us; the launch traced here: 637 us
  blocking collectives  204 us (32%)
  matrix products  191 us (30%)
  waiting for transfers between devices  140 us (22%)
  local copies, waits for them, and re-layouts  86.4 us (14%)
  between operations  14.1 us (2%)
    psum x1, blocking collectives, per_device(): total = lax.psum(flat, 'mem')  165 us
    dot_general x10, matrix products, accumulate(): lax.dot_general(row_table, lower, contract, preferred_element_type=jnp.fl...  113 us
    psum x1, waiting for transfers between devices, per_device(): weight_grad, bias_grad = lax.psum((local_grad, local_bias), ('grp', 'mem'))  85.7 us
    while x40, local copies, waits for them, and re-layouts  61.2 us
    all_gather x1, waiting for transfers between devices, per_device(): group = lax.all_gather(history, 'mem', axis=0, tiled=True)  54 us
    psum x1, blocking collectives, per_device(): weight_grad, bias_grad = lax.psum((local_grad, local_bias), ('grp', 'mem'))  39.3 us
    dot_general x10, matrix products, accumulate(): lax.dot_general(row_table, upper, contract, preferred_element_type=jnp.fl...  34.5 us
    dot_general x10, matrix products, accumulate(): jnp.einsum('tij,tjh->tih', piece, picked, preferred_element_type=jnp.floa...  28.5 us
  transfers between devices with their start and end apart: 2, of which 2 were waited for; matrix products, arithmetic and copies ran while one was open for 0% of the time, Pallas kernels for 0%

commit v1 on v0

--- a/solution.py
+++ b/solution.py
@@ -40,7 +40,9 @@
 
     dense = lax.fori_loop(0, count, accumulate, jnp.zeros((nblk, block * width), jnp.float32))
     flat = dense.reshape(nblk * block, width)
-    total = lax.psum(flat, "mem")
+    total = flat
+    for hop in (1, 2, 4):
+        total = total + lax.ppermute(total, "mem", [(dev, dev ^ hop) for dev in range(8)])
     summed = lax.dynamic_slice_in_dim(total, lax.axis_index("mem") * own_rows, own_rows, 0)
     merged = summed.astype(jnp.bfloat16)
     pre = jnp.dot(merged, weight, preferred_element_type=jnp.float32) + bias

time: 639 us -> 859 us (1.34)
  waiting for transfers between devices: 140 us -> 500 us
  blocking collectives: 204 us -> 38.5 us
  local copies, waits for them, and re-layouts: 86.4 us -> 108 us
    ppermute x0 -> x3, waiting for transfers between devices: none -> 357 us  [per_device(): lax.ppermute(total, 'mem', [(dev, dev ^ hop) for dev in range(8)])]
    psum x1 -> x0, blocking collectives: 165 us -> none  [per_device(): total = lax.psum(flat, 'mem')]
    while x40, local copies, waits for them, and re-layouts: 61.2 us -> 82.3 us
  transfers between devices with their start and end apart: 2 -> 5, of which waited for: 2 -> 5; matrix products, arithmetic and copies ran while one was open for 0% -> 0% of each run, Pallas kernels for 0% -> 0%
where the time goes in v1:
time: 859 us; the launch traced here: 858 us
  waiting for transfers between devices  500 us (58%)
  matrix products  185 us (22%)
  local copies, waits for them, and re-layouts  108 us (13%)
  blocking collectives  38.5 us (4%)
  between operations  14.1 us (2%)
    ppermute x3, waiting for transfers between devices, per_device(): lax.ppermute(total, 'mem', [(dev, dev ^ hop) for dev in range(8)])  357 us
    dot_general x10, matrix products, accumulate(): lax.dot_general(row_table, lower, contract, preferred_element_type=jnp.fl...  113 us
    psum x1, waiting for transfers between devices, per_device(): weight_grad, bias_grad = lax.psum((local_grad, local_bias), ('grp', 'mem'))  88.4 us
    while x40, local copies, waits for them, and re-layouts  82.3 us
    all_gather x1, waiting for transfers between devices, per_device(): group = lax.all_gather(history, 'mem', axis=0, tiled=True)  54 us
    psum x1, blocking collectives, per_device(): weight_grad, bias_grad = lax.psum((local_grad, local_bias), ('grp', 'mem'))  38.5 us
    dot_general x10, matrix products, accumulate(): jnp.einsum('tij,tjh->tih', piece, picked, preferred_element_type=jnp.floa...  28.5 us
    dot_general x10, matrix products, accumulate(): lax.dot_general(row_table, upper, contract, preferred_element_type=jnp.fl...  27.9 us
  transfers between devices with their start and end apart: 5, of which 5 were waited for; matrix products, arithmetic and copies ran while one was open for 0% of the time, Pallas kernels for 0%

profile of v1, /device:TPU:0, one launch (start us, length us, event | category | flops | bytes accessed | tf_op | source)
XLA Modules:
  0.0 857.6 jit_solution(5728018738325929931)
XLA Ops:
  8.0 54.0 %all-gather.2.cloned.1.call-done = bf16[4096,256]{1,0:T(8,128)(2,1)} async-done(((bf16[512,256]{1,0:T(8,128)(2,1)}), bf16[4096,256]{1,0:T(8,128)(2,1)}) %all-gather.2.cloned.1.call-update) | async-done | bytes 2097168 | tf_op jit(solution)/shard_map/all_gather | solution.py:12
  62.0 2.9 reshape.29
  64.8 281.1 %while.15 = (s32[]{:T(128)}, f32[32,32768]{1,0:T(8,128)}, s32[640]{0:T(1024)}, bf16[640,128,128]{2,1,0:T(8,128)(2,1)}, s32[640]{0:T(1024)}, /*index=5*/bf16[32,3...) while((s32[]{:T(128)}, f32[32,32768]{1,0:T(8,128)}, ...), condition=%wide.region_1.0_spmd.clone.clone, body=%wide.region_0.0_spmd.clone.clone.sunk | while | flops 955258880 | bytes 113248192 | solution.py:41
  68.0 2.9 fusion.31
  70.9 4.7 copy.15
  76.4 2.4 copy-done.1
  78.8 2.8 fusion.32
  81.6 10.3 %fusion.33 = f32[32,32768]{1,0:T(8,128)} fusion(f32[32,32768]{1,0:T(8,128)} %fusion.32, f32[64,32768]{1,0:T(8,128)} %bitcast.23, f32[32,32768]{1,0:T(8,128)} %get-tuple-element.235, pred[]{:T(512)S(6)} %compare.3, s32[64]{0:T(128)S(1)} %dynamic_slice.44), kind=kOutput, calls=%fused_computation.3.clone.1 | convolution fusion | flops 145754112 | bytes 20971776 | tf_op jit(solution)/shard_map/while/body/eval_jaxpr/dot_general | solution.py:36
  95.1 2.9 fusion.31
  97.9 4.7 copy.15
  103.5 2.4 copy-done.1
  105.9 2.8 fusion.32
  108.7 11.5 %fusion.33 = f32[32,32768]{1,0:T(8,128)} fusion(f32[32,32768]{1,0:T(8,128)} %fusion.32, f32[64,32768]{1,0:T(8,128)} %bitcast.23, f32[32,32768]{1,0:T(8,128)} %get-tuple-element.235, pred[]{:T(512)S(6)} %compare.3, s32[64]{0:T(128)S(1)} %dynamic_slice.44), kind=kOutput, calls=%fused_computation.3.clone.1 | convolution fusion | flops 145754112 | bytes 20971776 | tf_op jit(solution)/shard_map/while/body/eval_jaxpr/dot_general | solution.py:36
  123.3 2.9 fusion.31
  126.1 4.7 copy.15
  131.7 2.4 copy-done.1
  134.1 2.8 fusion.32
  136.9 11.5 %fusion.33 = f32[32,32768]{1,0:T(8,128)} fusion(f32[32,32768]{1,0:T(8,128)} %fusion.32, f32[64,32768]{1,0:T(8,128)} %bitcast.23, f32[32,32768]{1,0:T(8,128)} %get-tuple-element.235, pred[]{:T(512)S(6)} %compare.3, s32[64]{0:T(128)S(1)} %dynamic_slice.44), kind=kOutput, calls=%fused_computation.3.clone.1 | convolution fusion | flops 145754112 | bytes 20971776 | tf_op jit(solution)/shard_map/while/body/eval_jaxpr/dot_general | solution.py:36
  151.5 2.9 fusion.31
  154.4 4.7 copy.15
  159.9 2.4 copy-done.1
  162.3 2.8 fusion.32
  165.1 11.5 %fusion.33 = f32[32,32768]{1,0:T(8,128)} fusion(f32[32,32768]{1,0:T(8,128)} %fusion.32, f32[64,32768]{1,0:T(8,128)} %bitcast.23, f32[32,32768]{1,0:T(8,128)} %get-tuple-element.235, pred[]{:T(512)S(6)} %compare.3, s32[64]{0:T(128)S(1)} %dynamic_slice.44), kind=kOutput, calls=%fused_computation.3.clone.1 | convolution fusion | flops 145754112 | bytes 20971776 | tf_op jit(solution)/shard_map/while/body/eval_jaxpr/dot_general | solution.py:36
  179.7 2.9 fusion.31
  182.6 4.7 copy.15
  188.2 2.4 copy-done.1
  190.6 2.8 fusion.32
  193.3 11.5 %fusion.33 = f32[32,32768]{1,0:T(8,128)} fusion(f32[32,32768]{1,0:T(8,128)} %fusion.32, f32[64,32768]{1,0:T(8,128)} %bitcast.23, f32[32,32768]{1,0:T(8,128)} %get-tuple-element.235, pred[]{:T(512)S(6)} %compare.3, s32[64]{0:T(128)S(1)} %dynamic_slice.44), kind=kOutput, calls=%fused_computation.3.clone.1 | convolution fusion | flops 145754112 | bytes 20971776 | tf_op jit(solution)/shard_map/while/body/eval_jaxpr/dot_general | solution.py:36
  208.0 2.9 fusion.31
  210.8 4.7 copy.15
  216.4 2.4 copy-done.1
  218.8 2.8 fusion.32
  221.6 11.5 %fusion.33 = f32[32,32768]{1,0:T(8,128)} fusion(f32[32,32768]{1,0:T(8,128)} %fusion.32, f32[64,32768]{1,0:T(8,128)} %bitcast.23, f32[32,32768]{1,0:T(8,128)} %get-tuple-element.235, pred[]{:T(512)S(6)} %compare.3, s32[64]{0:T(128)S(1)} %dynamic_slice.44), kind=kOutput, calls=%fused_computation.3.clone.1 | convolution fusion | flops 145754112 | bytes 20971776 | tf_op jit(solution)/shard_map/while/body/eval_jaxpr/dot_general | solution.py:36
  236.2 2.9 fusion.31
  239.0 4.7 copy.15
  244.6 2.4 copy-done.1
  247.0 2.8 fusion.32
  249.8 11.5 %fusion.33 = f32[32,32768]{1,0:T(8,128)} fusion(f32[32,32768]{1,0:T(8,128)} %fusion.32, f32[64,32768]{1,0:T(8,128)} %bitcast.23, f32[32,32768]{1,0:T(8,128)} %get-tuple-element.235, pred[]{:T(512)S(6)} %compare.3, s32[64]{0:T(128)S(1)} %dynamic_slice.44), kind=kOutput, calls=%fused_computation.3.clone.1 | convolution fusion | flops 145754112 | bytes 20971776 | tf_op jit(solution)/shard_map/while/body/eval_jaxpr/dot_general | solution.py:36
  264.4 2.9 fusion.31
  267.3 4.7 copy.15
  272.8 2.4 copy-done.1
  275.2 2.8 fusion.32
  278.0 11.5 %fusion.33 = f32[32,32768]{1,0:T(8,128)} fusion(f32[32,32768]{1,0:T(8,128)} %fusion.32, f32[64,32768]{1,0:T(8,128)} %bitcast.23, f32[32,32768]{1,0:T(8,128)} %get-tuple-element.235, pred[]{:T(512)S(6)} %compare.3, s32[64]{0:T(128)S(1)} %dynamic_slice.44), kind=kOutput, calls=%fused_computation.3.clone.1 | convolution fusion | flops 145754112 | bytes 20971776 | tf_op jit(solution)/shard_map/while/body/eval_jaxpr/dot_general | solution.py:36
  292.6 2.9 fusion.31
  295.5 4.7 copy.15
  301.1 2.4 copy-done.1
  303.5 2.8 fusion.32
  306.3 11.5 %fusion.33 = f32[32,32768]{1,0:T(8,128)} fusion(f32[32,32768]{1,0:T(8,128)} %fusion.32, f32[64,32768]{1,0:T(8,128)} %bitcast.23, f32[32,32768]{1,0:T(8,128)} %get-tuple-element.235, pred[]{:T(512)S(6)} %compare.3, s32[64]{0:T(128)S(1)} %dynamic_slice.44), kind=kOutput, calls=%fused_computation.3.clone.1 | convolution fusion | flops 145754112 | bytes 20971776 | tf_op jit(solution)/shard_map/while/body/eval_jaxpr/dot_general | solution.py:36
  320.9 2.9 fusion.31
  323.7 4.7 copy.15
  329.3 2.4 copy-done.1
  331.7 2.8 fusion.32
  334.5 11.5 %fusion.33 = f32[32,32768]{1,0:T(8,128)} fusion(f32[32,32768]{1,0:T(8,128)} %fusion.32, f32[64,32768]{1,0:T(8,128)} %bitcast.23, f32[32,32768]{1,0:T(8,128)} %get-tuple-element.235, pred[]{:T(512)S(6)} %compare.3, s32[64]{0:T(128)S(1)} %dynamic_slice.44), kind=kOutput, calls=%fused_computation.3.clone.1 | convolution fusion | flops 145754112 | bytes 20971776 | tf_op jit(solution)/shard_map/while/body/eval_jaxpr/dot_general | solution.py:36
  345.9 4.9 reshape.30
  351.4 90.0 %collective-permute-done = f32[4096,256]{1,0:T(8,128)S(1)} collective-permute-done((f32[4096,256]{1,0:T(8,128)}, f32[4096,256]{1,0:T(8,128)S(1)}, u32[]{:S(2)}, u32[]{:S(2)}) %collective-permute-start) | collective-permute-done | bytes 4194336 | tf_op jit(solution)/shard_map/ppermute | solution.py:45
  441.4 2.7 add.69
  444.2 2.4 collective-permute-start.1
  446.6 88.7 %collective-permute-done.1 = f32[4096,256]{1,0:T(8,128)S(1)} collective-permute-done((f32[4096,256]{1,0:T(8,128)S(1)}, f32[4096,256]{1,0:T(8,128)S(1)}, u32[]{:S(2)}, u32[]{:S(2)}) %collective-permute-start.1) | collective-permute-done | bytes 4194336 | tf_op jit(solution)/shard_map/ppermute | solution.py:45
  535.3 2.5 add.70
  537.8 2.7 collective-permute-start.2
  540.5 178.3 %collective-permute-done.2 = f32[4096,256]{1,0:T(8,128)} collective-permute-done((f32[4096,256]{1,0:T(8,128)}, f32[4096,256]{1,0:T(8,128)}, u32[]{:S(2)}, u32[]{:S(2)}) %collective-permute-start.2) | collective-permute-done | bytes 4194336 | tf_op jit(solution)/shard_map/ppermute | solution.py:45
  722.3 38.5 %psum.15 = f32[256]{0:T(256)} all-reduce(f32[256]{0:T(256)S(1)} %get-tuple-element.184), channel_id=1, replica_groups=mesh['grp'=4,'mem'=8] {'grp','mem'}, use_global_device_ids=true, to_apply=%region_4.0 | all-reduce | flops 256 | bytes 2048 | tf_op jit(solution)/shard_map/psum | solution.py:57
  760.7 88.4 %all-reduce.2.cloned.1.call-done = f32[256,256]{1,0:T(8,128)} async-done(((f32[256,256]{1,0:T(8,128)}), f32[256,256]{1,0:T(8,128)}) %all-reduce.2.cloned.1.call-update) | async-done | bytes 262160 | tf_op jit(solution)/shard_map/psum | solution.py:57
  849.1 1.7 copy.23
  (65 shorter events, 44.3 us)
Async XLA Ops:
  7.2 712.9 %copy-start = (bf16[256,256]{1,0:T(8,128)(2,1)S(1)}, bf16[256,256]{1,0:T(8,128)(2,1)}, u32[]{:S(2)}) copy-start(bf16[256,256]{1,0:T(8,128)(2,1)} %param.13) | copy-start | bytes 393220
  7.2 54.8 %all-gather.2.cloned.1.call-start = ((), (), s32[]{:S(2)}) async-start(), calls=%async_computation | async-start | bytes 2359296 | tf_op jit(solution)/shard_map/all_gather | solution.py:12
  7.9 841.2 %all-reduce.2.cloned.1.call-start = ((), (), s32[]{:S(2)}) async-start(), calls=%async_computation.1 | async-start | bytes 524288 | tf_op jit(solution)/shard_map/psum | solution.py:57
  75.6 3.2 copy-start.1
  102.7 3.2 copy-start.1
  130.9 3.2 copy-start.1
  159.1 3.2 copy-start.1
  187.3 3.2 copy-start.1
  215.6 3.2 copy-start.1
  243.8 3.2 copy-start.1
  272.0 3.2 copy-start.1
  300.2 3.2 copy-start.1
  328.5 3.2 copy-start.1
  350.8 90.6 %collective-permute-start = (f32[4096,256]{1,0:T(8,128)}, f32[4096,256]{1,0:T(8,128)S(1)}, u32[]{:S(2)}, u32[]{:S(2)}) collective-permute-start(f32[4096,256]{1,0:T(8,128)} %reshape.30), channel_id=1, source_target_pairs={{0,1},{1,0},{2,3},{3,2},{4,5},{5,4},{6,7},{7,6},{8,9},{9,8},{10,11... | collective-permute-start | bytes 12582920 | tf_op jit(solution)/shard_map/ppermute | solution.py:45
  444.2 275.9 %copy-start.2 = (bf16[512,256]{1,0:T(8,128)(2,1)S(1)}, bf16[512,256]{1,0:T(8,128)(2,1)}, u32[]{:S(2)}) copy-start(bf16[512,256]{1,0:T(8,128)(2,1)} %param.15) | copy-start | bytes 786436
  444.2 275.9 %copy-start.3 = (f32[256]{0:T(256)S(1)}, f32[256]{0:T(256)}, u32[]{:S(2)}) copy-start(f32[256]{0:T(256)} %param.14) | copy-start | bytes 3076
  444.2 91.1 %collective-permute-start.1 = (f32[4096,256]{1,0:T(8,128)S(1)}, f32[4096,256]{1,0:T(8,128)S(1)}, u32[]{:S(2)}, u32[]{:S(2)}) collective-permute-start(f32[4096,256]{1,0:T(8,128)S(1)} %add.69), channel_id=1, source_target_pairs={{0,2},{1,3},{2,0},{3,1},{4,6},{5,7},{6,4},{7,5},{8,10},{9,11},{10,... | collective-permute-start | bytes 12582920 | tf_op jit(solution)/shard_map/ppermute | solution.py:45
  537.8 181.1 %collective-permute-start.2 = (f32[4096,256]{1,0:T(8,128)}, f32[4096,256]{1,0:T(8,128)}, u32[]{:S(2)}, u32[]{:S(2)}) collective-permute-start(f32[4096,256]{1,0:T(8,128)} %add.70), channel_id=1, source_target_pairs={{0,4},{1,5},{2,6},{3,7},{4,0},{5,1},{6,2},{7,3},{8,12},{9,13},{10,... | collective-permute-start | bytes 12582920 | tf_op jit(solution)/shard_map/ppermute | solution.py:45
Sparse Core Ops, SparseCore 0:
  10.1 51.7 all-gather.1
  722.4 126.6 all-reduce.1
